TPU v7x, 32 devices: a whole 2x2x4 slice. The times are simulated.
32 devices in a mesh: replica: 4 (over y, x), fsdp: 8 (over z, core).
Axes of the slice: x: 2, y: 2, z: 4, core: 2. Of those that a mesh axis runs over, the one named last changes fastest.
Arguments:
- hidden_in: bfloat16 [8192, 1024], P(('replica', 'fsdp')), may hold values from -8 to 8
- seq_lengths: int32 [32, 4], P(('replica', 'fsdp')), may hold values from 0 to 256, as said below
- routes: int32 [8192, 8], P(('replica', 'fsdp')), may hold values from 0 to 15, all different within a row; in each aligned block of 256 rows (0 to 255, 256 to 511, ...) at most 144 rows name the same one
- norm1_gain: bfloat16 [1024], P('fsdp'), may hold values from 0.25 to 1.75
- w_query: bfloat16 [1024, 1024], P('fsdp'), may hold values from -1 to 1
- w_key: bfloat16 [1024, 512], P('fsdp'), may hold values from -1 to 1
- w_value: bfloat16 [1024, 512], P('fsdp'), may hold values from -0.1875 to 0.1875
- w_output: bfloat16 [1024, 1024], P('fsdp'), may hold values from -6 to 6
- norm2_gain: bfloat16 [1024], P('fsdp'), may hold values from 0.25 to 1.75
- w_router: bfloat16 [1024, 16], P('fsdp'), may hold values from -3 to 3
- expert_weights: bfloat16 [16, 1536, 1024], P('fsdp'), may hold values from -3 to 3
- out_cotangent: bfloat16 [8192, 1024], P(('replica', 'fsdp')), may hold values from -6 to 6
Outputs:
- layer_out: bfloat16 [8192, 1024], P(('replica', 'fsdp'))
- grad_in: float32 [8192, 1024], P(('replica', 'fsdp'))
- grad_norm1: float32 [1024], P('fsdp')
- grad_query: float32 [1024, 1024], P('fsdp')
- grad_key: float32 [1024, 512], P('fsdp')
- grad_value: float32 [1024, 512], P('fsdp')
- grad_output: float32 [1024, 1024], P('fsdp')
- grad_norm2: float32 [1024], P('fsdp')
- grad_router: float32 [1024, 16], P('fsdp')
- grad_experts: float32 [16, 1536, 1024], P('fsdp')
Inputs may be any that keep to these rules, and one draw needn't show every extreme that they name: `seq_lengths`: each row sums to 256; a length may be 0; some row holds one sequence of 256. `routes`: A token's experts differ; among the rows of one device no expert is named more than 144 times, a bound that some block reaches.
All inputs are finite; a program needn't handle non-finite values.
Results may differ from a plain program's by a relative error of at most 0.015.
The roundings to bfloat16 on the way count: a program that leaves them out, or rounds other values in their place, can miss the bound.
Values may be sent and summed in bfloat16 or wider, within the bound.
A program may use at most 384 MiB of HBM per device.

v0:
```python
import jax
import jax.numpy as jnp
from jax import lax
from jax.sharding import PartitionSpec as P

D = 1024
H = 16
KVH = 8
HD = 64
FF = 512
TOPK = 8
E = 16
CAP = 144
norm_eps = 1e-06
score_scale = 0.015625
residual_scale = 0.22
rope_base = 10000.0
masked_score = -1e30


def inverse_rms(vector):
    return lax.rsqrt(jnp.mean(vector * vector, axis=-1, keepdims=True) + norm_eps)


def rms_back(vector, factor, gain_full, incoming):
    scaled = incoming * gain_full
    grad_gain = jnp.sum(incoming * vector * factor, axis=0)
    grad_vector = factor * scaled - vector * factor**3 * jnp.mean(
        scaled * vector, axis=-1, keepdims=True
    )
    return (grad_vector, grad_gain)


def rotate(vector, cosines, sine_table):
    half_size = vector.shape[-1] // 2
    turned = jnp.concatenate([-vector[..., half_size:], vector[..., :half_size]], axis=-1)
    return vector * cosines[:, None, :] + turned * sine_table[:, None, :]


def expert_forward(slot_inputs, weight_rows):
    gate_pre = jnp.einsum(
        "ecd,efd->ecf", slot_inputs, weight_rows[:, :FF], preferred_element_type=jnp.float32
    )
    up_pre = jnp.einsum(
        "ecd,efd->ecf", slot_inputs, weight_rows[:, FF : 2 * FF], preferred_element_type=jnp.float32
    )
    hidden_act = (jax.nn.silu(gate_pre) * up_pre).astype(jnp.bfloat16)
    produced = jnp.einsum(
        "ecf,efd->ecd", hidden_act, weight_rows[:, 2 * FF :], preferred_element_type=jnp.float32
    )
    return (produced.astype(jnp.bfloat16), gate_pre, up_pre)


def expert_backward(slot_grads, gate_pre, up_pre, weight_rows):
    sigmoid_gate = jax.nn.sigmoid(gate_pre)
    grad_act = jnp.einsum(
        "ecd,efd->ecf", slot_grads, weight_rows[:, 2 * FF :], preferred_element_type=jnp.float32
    )
    grad_gate = (
        grad_act * up_pre * (sigmoid_gate * (1.0 + gate_pre * (1.0 - sigmoid_gate)))
    ).astype(jnp.bfloat16)
    grad_up = (grad_act * jax.nn.silu(gate_pre)).astype(jnp.bfloat16)
    grad_rows = jnp.einsum(
        "ecf,efd->ecd", grad_gate, weight_rows[:, :FF], preferred_element_type=jnp.float32
    )
    grad_rows = grad_rows + jnp.einsum(
        "ecf,efd->ecd", grad_up, weight_rows[:, FF : 2 * FF], preferred_element_type=jnp.float32
    )
    return (grad_gate, grad_up, grad_rows.astype(jnp.bfloat16))


def expert_grads(slot_inputs, slot_grads, gate_pre, up_pre, grad_gate, grad_up):
    hidden_act = (jax.nn.silu(gate_pre) * up_pre).astype(jnp.bfloat16)
    return jnp.concatenate(
        [
            jnp.einsum("ecf,ecd->efd", grad_gate, slot_inputs, preferred_element_type=jnp.float32),
            jnp.einsum("ecf,ecd->efd", grad_up, slot_inputs, preferred_element_type=jnp.float32),
            jnp.einsum("ecf,ecd->efd", hidden_act, slot_grads, preferred_element_type=jnp.float32),
        ],
        axis=1,
    )


def body(
    hidden_in,
    seq_lengths,
    routes,
    norm1_gain,
    w_query,
    w_key,
    w_value,
    w_output,
    norm2_gain,
    w_router,
    expert_weights,
    out_cotangent,
):
    gain_one, query_w, key_w, value_w, output_w, gain_two, router_w = (
        lax.all_gather(norm1_gain, "fsdp", axis=0, tiled=True),
        lax.all_gather(w_query, "fsdp", axis=0, tiled=True),
        lax.all_gather(w_key, "fsdp", axis=0, tiled=True),
        lax.all_gather(w_value, "fsdp", axis=0, tiled=True),
        lax.all_gather(w_output, "fsdp", axis=0, tiled=True),
        lax.all_gather(norm2_gain, "fsdp", axis=0, tiled=True),
        lax.all_gather(w_router, "fsdp", axis=0, tiled=True),
    )
    tokens = hidden_in.shape[0]
    group = H // KVH
    block_rows = min(512, tokens)
    token_index = jnp.arange(tokens, dtype=jnp.int32)
    seq_ends = jnp.cumsum(seq_lengths[0])
    passed = token_index[:, None] >= seq_ends[None, :]
    segment = jnp.sum(passed.astype(jnp.int32), axis=1)
    position = token_index - jnp.max(jnp.where(passed, seq_ends[None, :], 0), axis=1)
    frequency = rope_base ** (-jnp.arange(0, HD, 2, dtype=jnp.float32) / HD)
    angles = position.astype(jnp.float32)[:, None] * frequency[None, :]
    angles = jnp.concatenate([angles, angles], axis=1)
    cosines = jnp.cos(angles)
    sine_table = jnp.sin(angles)
    allowed = (segment[:, None] == segment[None, :]) & (
        token_index[None, :] <= token_index[:, None]
    )
    source = hidden_in.astype(jnp.float32)
    factor_one = inverse_rms(source)
    gain_first = gain_one.astype(jnp.float32)
    normed = (source * factor_one * gain_first).astype(jnp.bfloat16)
    query_rot = rotate(
        jnp.dot(normed, query_w, preferred_element_type=jnp.float32).reshape(tokens, H, HD),
        cosines,
        sine_table,
    )
    query_rot = query_rot.astype(jnp.bfloat16).reshape(tokens, KVH, group, HD)
    key_rot = rotate(
        jnp.dot(normed, key_w, preferred_element_type=jnp.float32).reshape(tokens, KVH, HD),
        cosines,
        sine_table,
    )
    key_rot = key_rot.astype(jnp.bfloat16)
    value_rows = (
        jnp.dot(normed, value_w, preferred_element_type=jnp.float32)
        .astype(jnp.bfloat16)
        .reshape(tokens, KVH, HD)
    )

    def block_scores():
        raw_scores = (
            jnp.einsum("qkgd,tkd->kgqt", query_rot, key_rot, preferred_element_type=jnp.float32)
            * score_scale
        )
        return jnp.where(allowed[None, None], raw_scores, masked_score)

    scores = block_scores()
    row_max = jnp.max(scores, axis=-1, keepdims=True)
    shifted = jnp.exp(scores - row_max)
    row_total = jnp.sum(shifted, axis=-1, keepdims=True)
    weights = (shifted / row_total).astype(jnp.bfloat16)
    mixed_parts = jnp.einsum(
        "kgqt,tkd->qkgd", weights, value_rows, preferred_element_type=jnp.float32
    )
    log_totals = [row_max + jnp.log(row_total)]
    mixed = mixed_parts.reshape(tokens, H * HD).astype(jnp.bfloat16)
    after = source + residual_scale * jnp.dot(mixed, output_w, preferred_element_type=jnp.float32)
    factor_two = inverse_rms(after)
    gain_second = gain_two.astype(jnp.float32)
    normed_two = (after * factor_two * gain_second).astype(jnp.bfloat16)
    logits = jnp.dot(normed_two, router_w, preferred_element_type=jnp.float32)
    route_hits = (routes[:, :, None] == jnp.arange(E, dtype=jnp.int32)[None, None, :]).astype(
        jnp.float32
    )
    chosen = jnp.sum(route_hits * logits[:, None, :], axis=2)
    gate_probs = jax.nn.softmax(chosen, axis=1)
    flat_routes = routes.reshape(-1)
    flat_hits = (flat_routes[:, None] == jnp.arange(E, dtype=jnp.int32)[None, :]).astype(jnp.int32)
    slot_rank = jnp.sum((jnp.cumsum(flat_hits, axis=0) - flat_hits) * flat_hits, axis=1)
    slot_ids = flat_routes * CAP + slot_rank
    numbered = jnp.arange(tokens * TOPK, dtype=jnp.int32) + 1
    slot_owner = jnp.zeros((E * CAP,), jnp.int32).at[slot_ids].set(numbered) - 1
    filled = slot_owner >= 0
    owner_rows = jnp.maximum(slot_owner, 0)
    zero_half = jnp.zeros((), jnp.bfloat16)
    slot_inputs = jnp.where(filled[:, None], normed_two[owner_rows // TOPK], zero_half).reshape(
        E, CAP, D
    )
    produced, gate_pre, up_pre = expert_forward(
        slot_inputs, lax.all_gather(expert_weights, "fsdp", axis=0, tiled=True)
    )
    picked = produced.reshape(E * CAP, D)[slot_ids].reshape(tokens, TOPK, D)
    mixture = jnp.einsum("tk,tkd->td", gate_probs, picked, preferred_element_type=jnp.float32)
    layer_out = (after + residual_scale * mixture).astype(jnp.bfloat16)
    grad_out = out_cotangent.astype(jnp.float32)
    grad_moe = residual_scale * grad_out
    grad_gates = jnp.einsum("td,tkd->tk", grad_moe, picked, preferred_element_type=jnp.float32)
    grad_chosen = gate_probs * (
        grad_gates - jnp.sum(gate_probs * grad_gates, axis=1, keepdims=True)
    )
    grad_logits = jnp.sum(route_hits * grad_chosen[:, :, None], axis=1).astype(jnp.bfloat16)
    grad_router = jnp.einsum(
        "td,te->de", normed_two, grad_logits, preferred_element_type=jnp.float32
    )
    grad_picked = (
        (gate_probs[:, :, None] * grad_moe[:, None, :])
        .astype(jnp.bfloat16)
        .reshape(tokens * TOPK, D)
    )
    slot_grads = jnp.where(filled[:, None], grad_picked[owner_rows], zero_half).reshape(E, CAP, D)
    grad_gate, grad_up, grad_rows = expert_backward(
        slot_grads, gate_pre, up_pre, lax.all_gather(expert_weights, "fsdp", axis=0, tiled=True)
    )
    grad_expert_shard = lax.psum_scatter(
        expert_grads(slot_inputs, slot_grads, gate_pre, up_pre, grad_gate, grad_up),
        "fsdp",
        scatter_dimension=0,
        tiled=True,
    )
    returned = grad_rows.reshape(E * CAP, D)[slot_ids].reshape(tokens, TOPK, D)
    grad_normed_two = jnp.einsum(
        "te,de->td", grad_logits, router_w, preferred_element_type=jnp.float32
    )
    grad_normed_two = grad_normed_two + jnp.sum(returned, axis=1, dtype=jnp.float32)
    grad_after_norm, grad_gain_two = rms_back(after, factor_two, gain_second, grad_normed_two)
    grad_after = grad_out + grad_after_norm
    grad_branch = (residual_scale * grad_after).astype(jnp.bfloat16)
    grad_output_w = jnp.einsum("tc,td->cd", mixed, grad_branch, preferred_element_type=jnp.float32)
    grad_mixed = jnp.einsum("td,cd->tc", grad_branch, output_w, preferred_element_type=jnp.float32)
    grad_mixed = grad_mixed.astype(jnp.bfloat16).reshape(tokens, KVH, group, HD)
    query_parts = []
    grad_key_rot = jnp.zeros((tokens, KVH, HD), jnp.float32)
    grad_value_rows = jnp.zeros((tokens, KVH, HD), jnp.float32)
    for number, offset in enumerate(range(0, tokens, block_rows)):
        scores = block_scores()
        weights_full = jnp.exp(scores - log_totals[number])
        grad_weights = jnp.einsum(
            "qkgd,tkd->kgqt", grad_mixed, value_rows, preferred_element_type=jnp.float32
        )
        grad_scores = weights_full * (
            grad_weights - jnp.sum(weights_full * grad_weights, axis=-1, keepdims=True)
        )
        grad_scores = grad_scores.astype(jnp.bfloat16)
        query_parts.append(
            jnp.einsum("kgqt,tkd->qkgd", grad_scores, key_rot, preferred_element_type=jnp.float32)
            * score_scale
        )
        grad_key_rot = (
            jnp.einsum("kgqt,qkgd->tkd", grad_scores, query_rot, preferred_element_type=jnp.float32)
            * score_scale
        )
        grad_value_rows = jnp.einsum(
            "kgqt,qkgd->tkd",
            weights_full.astype(jnp.bfloat16),
            grad_mixed,
            preferred_element_type=jnp.float32,
        )
    grad_query_rows = rotate(query_parts[0].reshape(tokens, H, HD), cosines, -sine_table)
    grad_query_rows = grad_query_rows.astype(jnp.bfloat16).reshape(tokens, H * HD)
    grad_key_rows = (
        rotate(grad_key_rot, cosines, -sine_table).astype(jnp.bfloat16).reshape(tokens, KVH * HD)
    )
    grad_value_flat = grad_value_rows.astype(jnp.bfloat16).reshape(tokens, KVH * HD)
    grad_query_w = jnp.einsum(
        "td,tc->dc", normed, grad_query_rows, preferred_element_type=jnp.float32
    )
    grad_key_w = jnp.einsum("td,tc->dc", normed, grad_key_rows, preferred_element_type=jnp.float32)
    grad_value_w = jnp.einsum(
        "td,tc->dc", normed, grad_value_flat, preferred_element_type=jnp.float32
    )
    grad_normed = jnp.einsum(
        "tc,dc->td", grad_query_rows, query_w, preferred_element_type=jnp.float32
    )
    grad_normed = grad_normed + jnp.einsum(
        "tc,dc->td", grad_key_rows, key_w, preferred_element_type=jnp.float32
    )
    grad_normed = grad_normed + jnp.einsum(
        "tc,dc->td", grad_value_flat, value_w, preferred_element_type=jnp.float32
    )
    grad_input_norm, grad_gain_one = rms_back(source, factor_one, gain_first, grad_normed)
    grad_in = grad_after + grad_input_norm
    (
        shard_gain_one,
        shard_query,
        shard_key,
        shard_value,
        shard_output,
        shard_gain_two,
        shard_router,
    ) = (
        lax.psum_scatter(grad_gain_one, "fsdp", scatter_dimension=0, tiled=True),
        lax.psum_scatter(grad_query_w, "fsdp", scatter_dimension=0, tiled=True),
        lax.psum_scatter(grad_key_w, "fsdp", scatter_dimension=0, tiled=True),
        lax.psum_scatter(grad_value_w, "fsdp", scatter_dimension=0, tiled=True),
        lax.psum_scatter(grad_output_w, "fsdp", scatter_dimension=0, tiled=True),
        lax.psum_scatter(grad_gain_two, "fsdp", scatter_dimension=0, tiled=True),
        lax.psum_scatter(grad_router, "fsdp", scatter_dimension=0, tiled=True),
    )
    summed = lax.psum(
        (
            shard_gain_one,
            shard_query,
            shard_key,
            shard_value,
            shard_output,
            shard_gain_two,
            shard_router,
            grad_expert_shard,
        ),
        "replica",
    )
    return (
        layer_out,
        grad_in,
        summed[0],
        summed[1],
        summed[2],
        summed[3],
        summed[4],
        summed[5],
        summed[6],
        summed[7],
    )


def solution(mesh):
    return jax.shard_map(
        body,
        mesh=mesh,
        in_specs=(
            P(("replica", "fsdp"), None),
            P(("replica", "fsdp"), None),
            P(("replica", "fsdp"), None),
            P("fsdp"),
            P("fsdp", None),
            P("fsdp", None),
            P("fsdp", None),
            P("fsdp", None),
            P("fsdp"),
            P("fsdp", None),
            P("fsdp", None, None),
            P(("replica", "fsdp"), None),
        ),
        out_specs=(
            P(("replica", "fsdp"), None),
            P(("replica", "fsdp"), None),
            P("fsdp"),
            P("fsdp", None),
            P("fsdp", None),
            P("fsdp", None),
            P("fsdp", None),
            P("fsdp"),
            P("fsdp", None),
            P("fsdp", None, None),
        ),
        check_vma=False,
    )
```

profile of v0, /device:TPU:0, one launch (start us, length us, event | category | flops | bytes accessed | tf_op | source)
XLA Modules:
  0.0 2149.8 jit_solution(16897767280440720643)
XLA Ops:
  11.1 13.5 all-gather
  24.6 8.6 all-gather.1
  33.7 4.5 reduce-window.19
  39.0 8.1 scatter_custom_fusion
  47.2 12.7 all_gather.31
  64.8 1.9 fusion.105
  66.9 21.5 all-gather.12.cloned.1.call-done
  88.4 2.6 fusion.103
  95.8 22.7 %all-gather.14.cloned.1.call-done = bf16[1024,1024]{1,0:T(8,128)(2,1)} async-done(((bf16[128,1024]{1,0:T(8,128)(2,1)}), bf16[1024,1024]{1,0:T(8,128)(2,1)}) %all-gather.14.cloned.1.call-update) | async-done | bytes 2097168 | tf_op jit(solution)/shard_map/all_gather | solution.py:103
  118.5 2.4 multiply_reduce_fusion.2
  122.1 8.3 gather_fusion
  131.3 415.6 %all-gather.16.cloned.1.call-done = bf16[16,1536,1024]{2,1,0:T(8,128)(2,1)} async-done(((bf16[2,1536,1024]{2,1,0:T(8,128)(2,1)}), bf16[16,1536,1024]{2,1,0:T(8,128)(2,1)}) %all-gather.16.cloned.1.call-update) | async-done | bytes 50331664 | tf_op jit(solution)/shard_map/all_gather | solution.py:185
  546.9 11.5 fusion.10
  558.4 13.0 multiply_convert_fusion.2
  571.4 11.4 fusion.26
  582.8 14.4 gather_fusion.1
  597.2 4.5 fusion.17
  602.2 4.4 fusion.19
  606.7 2.4 fusion.12
  609.1 13.7 gather_fusion.2
  622.8 14.3 multiply_convert_fusion.1
  637.1 12.3 fusion.4
  649.4 12.3 add_convert_fusion
  661.7 13.9 gather_fusion.3
  675.6 5.6 convert_reduce_fusion
  687.5 3.0 fusion.45
  691.2 2.0 fusion.97
  693.2 3.4 fusion.14
  700.8 1.9 fusion.99
  702.8 4.2 fusion.70
  707.0 2.1 convolution_multiply_fusion
  710.3 2.9 fusion.101
  713.1 19.0 fusion.21
  732.5 19.3 fusion.25
  751.8 18.2 fusion.24
  770.0 67.1 %pad_maximum_fusion = f32[16,1536,1024]{2,1,0:T(8,128)} fusion(f32[16,512,1024]{2,1,0:T(8,128)} %fusion.21, f32[16,512,1024]{2,1,0:T(8,128)} %fusion.24, f32[16,512,1024]{2,1,0:T(8,128)} %fusion.25), kind=kLoop, calls=%fused_computation.5 | loop fusion | flops 50331648 | bytes 201326592 | tf_op jit(solution)/shard_map/concatenate | solution.py:74
  839.1 27.1 %reduce-scatter.7.cloned.1.call-done = f32[128,1024]{1,0:T(8,128)} async-done(((f32[1024,1024]{1,0:T(8,128)}), f32[128,1024]{1,0:T(8,128)}) %reduce-scatter.7.cloned.1.call-update) | async-done | bytes 524304 | tf_op jit(solution)/shard_map/reduce_scatter | solution.py:287
  866.2 955.4 %reduce-scatter.17.cloned.1.call-done = f32[2,1536,1024]{2,1,0:T(8,128)} async-done(((f32[16,1536,1024]{2,1,0:T(8,128)}), f32[2,1536,1024]{2,1,0:T(8,128)}) %reduce-scatter.17.cloned.1.call-update) | async-done | bytes 12582928 | tf_op jit(solution)/shard_map/reduce_scatter | solution.py:209
  1823.5 2.4 fusion.111
  1826.0 1.7 convolution_add_fusion.2
  1827.7 1.9 fusion.56
  1829.7 13.9 all-reduce.2
  1845.1 7.9 reduce-scatter.15.cloned.1.call-done
  1852.9 11.0 all-reduce.3
  1863.9 259.5 %all-reduce.7.cloned.1.call-done = (f32[128,1024]{1,0:T(8,128)}, f32[128,512]{1,0:T(8,128)}, f32[128,512]{1,0:T(8,128)}, f32[128,1024]{1,0:T(8,128)}, f32[2,1536,1024]{2,1,0:T(8,128)}) async-done(((f32[128,1024]{1,0:T(8,128)}, f32[128,512]{1,0:T(8,128)}, f32[128,512]{1,0:T(8,128)}, f32[128,1024]{1,0:T(8,128)}, f32[2,1536,1024]{2,1,0:T(8,128)}), (f32[128,1024]{1,0:T(8,128)}, f32[128,512]{1,0:T(8,128)}, ...) | async-done | bytes 14155792 | tf_op jit(solution)/shard_map/psum | solution.py:294
  2123.4 1.9 copy.103
  2128.6 1.9 copy.106
  2130.5 12.1 copy.107
  (221 shorter events, 37.9 us)
Async XLA Ops:
  7.2 17.4 copy-start.56
  7.2 26.3 %copy-start.57 = (s32[1,4]{1,0:T(1,128)S(1)}, s32[1,4]{1,0:T(1,128)}, u32[]{:S(2)}) copy-start(s32[1,4]{1,0:T(1,128)} %param.13) | copy-start | bytes 52
  7.2 40.0 %copy-start.54 = (bf16[128,16]{0,1:T(8,128)(2,1)S(1)}, bf16[128,16]{0,1:T(8,128)(2,1)}, u32[]{:S(2)}) copy-start(bf16[128,16]{0,1:T(8,128)(2,1)} %param.21) | copy-start | bytes 12292
  7.2 53.7 %copy-start.4 = (bf16[256,1024]{1,0:T(8,128)(2,1)S(1)}, bf16[256,1024]{1,0:T(8,128)(2,1)}, u32[]{:S(2)}) copy-start(bf16[256,1024]{1,0:T(8,128)(2,1)} %param.12) | copy-start | bytes 1572868
  7.2 55.7 %all-gather.8.cloned.1.call-start = ((), (), s32[]{:S(2)}) async-start(), calls=%async_computation.6 | async-start | bytes 1179648 | tf_op jit(solution)/shard_map/all_gather | solution.py:102
  8.0 56.8 %all-gather.10.cloned.1.call-start = ((), (), s32[]{:S(2)}) async-start(), calls=%async_computation.7 | async-start | bytes 1179648 | tf_op jit(solution)/shard_map/all_gather | solution.py:101
  8.7 79.7 %all-gather.12.cloned.1.call-start = ((), (), s32[]{:S(2)}) async-start(), calls=%async_computation.8 | async-start | bytes 2359296 | tf_op jit(solution)/shard_map/all_gather | solution.py:100
  9.5 52.4 %copy-start.15 = (bf16[256,1024]{1,0:T(8,128)(2,1)S(1)}, bf16[256,1024]{1,0:T(8,128)(2,1)}, u32[]{:S(2)}) copy-start(bf16[256,1024]{1,0:T(8,128)(2,1)} %param.23) | copy-start | bytes 1572868
  9.5 109.0 %all-gather.14.cloned.1.call-start = ((), (), s32[]{:S(2)}) async-start(), calls=%async_computation.9 | async-start | bytes 2359296 | tf_op jit(solution)/shard_map/all_gather | solution.py:103
  10.0 536.9 %all-gather.16.cloned.1.call-start = ((), (), s32[]{:S(2)}) async-start(), calls=%async_computation.10 | async-start | bytes 56623104 | tf_op jit(solution)/shard_map/all_gather | solution.py:185
  10.6 828.4 %reduce-scatter.11.cloned.1.call-start = ((), (), s32[]{:S(2)}) async-start(), calls=%async_computation.13 | async-start | bytes 2359296 | tf_op jit(solution)/shard_map/reduce_scatter | solution.py:289
  24.5 63.9 %copy-start.38 = (f32[8,1,128]{2,1,0:T(1,128)}, f32[8,1,128]{2,1,0:T(1,128)S(1)}, u32[]{:S(2)}) copy-start(f32[8,1,128]{2,1,0:T(1,128)S(1)} %convert_element_type.151) | copy-start | bytes 12292
  33.2 88.4 %copy-start.44 = (f32[8,1,128]{2,1,0:T(1,128)}, f32[8,1,128]{2,1,0:T(1,128)S(1)}, u32[]{:S(2)}) copy-start(f32[8,1,128]{2,1,0:T(1,128)S(1)} %convert_element_type.152) | copy-start | bytes 12292
  59.9 70.4 %copy-start.34 = (bf16[1024,16]{0,1:T(8,128)(2,1)}, bf16[1024,16]{0,1:T(8,128)(2,1)S(1)}, u32[]{:S(2)}) copy-start(bf16[1024,16]{0,1:T(8,128)(2,1)S(1)} %all_gather.31) | copy-start | bytes 98308
  61.0 30.1 %copy-start.30 = (f32[256,64]{0,1:T(8,128)}, f32[256,64]{0,1:T(8,128)S(1)}, u32[]{:S(2)}) copy-start(f32[256,64]{0,1:T(8,128)S(1)} %get-tuple-element.43) | copy-start | bytes 196612
  61.8 26.6 %copy-start.46 = (f32[256]{0:T(256)}, f32[256]{0:T(256)S(1)}, u32[]{:S(2)}) copy-start(f32[256]{0:T(256)S(1)} %get-tuple-element.47) | copy-start | bytes 3076
  64.8 28.8 %copy-start.29 = (bf16[256,512]{0,1:T(8,128)(2,1)}, bf16[256,512]{0,1:T(8,128)(2,1)S(1)}, u32[]{:S(2)}) copy-start(bf16[256,512]{0,1:T(8,128)(2,1)S(1)} %copy.66) | copy-start | bytes 786436
  66.9 26.0 %copy-start.24 = (bf16[256,8,64,1]{0,2,3,1:T(8,128)(2,1)}, bf16[256,8,64,1]{0,2,3,1:T(8,128)(2,1)S(1)}, u32[]{:S(2)}) copy-start(bf16[256,8,64,1]{0,2,3,1:T(8,128)(2,1)S(1)} %fusion.68) | copy-start | bytes 786436
  95.8 34.6 %copy-start.28 = (bf16[8,64,2,256]{3,1,2,0:T(8,128)(2,1)}, bf16[8,64,2,256]{3,1,2,0:T(8,128)(2,1)S(1)}, u32[]{:S(2)}) copy-start(bf16[8,64,2,256]{3,1,2,0:T(8,128)(2,1)S(1)} %fusion.41) | copy-start | bytes 1572868
  121.6 8.8 copy-start.50
  122.1 8.3 copy-start
  571.4 11.4 copy-start.14
  582.8 14.4 copy-start.33
  602.0 79.2 %copy-start.42 = (bf16[256,16]{0,1:T(8,128)(2,1)}, bf16[256,16]{0,1:T(8,128)(2,1)S(1)}, u32[]{:S(2)}) copy-start(bf16[256,16]{0,1:T(8,128)(2,1)S(1)} %select_reduce_fusion) | copy-start | bytes 24580
  637.1 12.3 copy-start.7
  675.5 5.7 copy-start.12
  675.5 5.7 copy-start.35
  675.5 5.7 copy-start.45
  675.5 5.7 copy-start.51
  675.6 6.9 copy-start.16
  675.6 6.9 copy-start.21
  675.6 6.9 copy-start.53
  684.7 6.5 copy-start.5
  684.7 6.5 copy-start.39
  684.7 6.5 copy-start.47
  693.2 145.9 %reduce-scatter.9.cloned.1.call-start = ((), (), s32[]{:S(2)}) async-start(), calls=%async_computation.12 | async-start | bytes 2359296 | tf_op jit(solution)/shard_map/reduce_scatter | solution.py:288
  702.7 136.4 %reduce-scatter.13.cloned.1.call-start = ((), (), s32[]{:S(2)}) async-start(), calls=%async_computation.14 | async-start | bytes 4718592 | tf_op jit(solution)/shard_map/reduce_scatter | solution.py:290
  706.9 159.3 %reduce-scatter.7.cloned.1.call-start = ((), (), s32[]{:S(2)}) async-start(), calls=%async_computation.11 | async-start | bytes 4718592 | tf_op jit(solution)/shard_map/reduce_scatter | solution.py:287
  732.2 1089.4 %reduce-scatter.17.cloned.1.call-start = ((), (), s32[]{:S(2)}) async-start(), calls=%async_computation.16 | async-start | bytes 113246208 | tf_op jit(solution)/shard_map/reduce_scatter | solution.py:209
  837.2 1015.8 %reduce-scatter.15.cloned.1.call-start = ((), (), s32[]{:S(2)}) async-start(), calls=%async_computation.15 | async-start | bytes 73728 | tf_op jit(solution)/shard_map/reduce_scatter | solution.py:292
  839.0 1284.4 %all-reduce.7.cloned.1.call-start = ((), (), s32[]{:S(2)}) async-start(), calls=%async_computation.17 | async-start | bytes 28311552 | tf_op jit(solution)/shard_map/psum | solution.py:294
  1821.6 6.1 copy-start.6
  1821.6 6.1 copy-start.23
  1821.6 6.1 copy-start.40
  1821.7 6.1 copy-start.48
  1823.5 6.2 copy-start.49
  1823.5 20.3 copy-start.10
  1823.5 20.3 copy-start.52
  (23 other events, 47.3 us)
Sparse Core Ops, SparseCore 0:
  9.7 24.7 all-gather.7
  36.1 21.8 all-gather.9
  59.6 28.7 all-gather.11
  89.9 28.5 all-gather.13
  120.0 426.8 all-gather.15
  693.3 33.9 reduce-scatter.10
  729.6 34.5 reduce-scatter.8
  766.5 48.5 reduce-scatter.12
  818.0 48.1 reduce-scatter.6
  868.4 953.1 reduce-scatter.16
  1824.5 28.3 reduce-scatter.14
  1857.1 266.2 all-reduce.6
where the time goes:
time: 2160 us; the launch traced here: 2150 us
  waiting for transfers between devices  1710 us (79%)
  matrix products  181 us (8%)
  local copies, waits for them, and re-layouts  90.1 us (4%)
  other arithmetic  89.7 us (4%)
  blocking collectives  59.8 us (3%)
    reduce_scatter x1, waiting for transfers between devices, body(): lax.psum_scatter(expert_grads(slot_inputs, slot_grads, gate_pre, up_pre,...  955 us
    all_gather x1, waiting for transfers between devices, body(): lax.all_gather(expert_weights, 'fsdp', axis=0, tiled=True)  416 us
    psum x1, waiting for transfers between devices, body(): lax.psum((shard_gain_one, shard_query, shard_key, shard_value, shard_outp...  259 us
    concatenate x1, other arithmetic, expert_grads(): jnp.concatenate([jnp.einsum('ecf,ecd->efd', grad_gate, slot_inputs, prefe...  67.1 us
  transfers between devices with their start and end apart: 12, of which 7 were waited for; matrix products, arithmetic and copies ran while one was open for 9% of the time, Pallas kernels for 0%

commit v1 on v0

--- a/solution.py
+++ b/solution.py
@@ -1,3 +1,4 @@
+import functools
 import jax
 import jax.numpy as jnp
 from jax import lax
@@ -16,6 +17,35 @@
 residual_scale = 0.22
 rope_base = 10000.0
 masked_score = -1e30
+
+
+def track_packet_for(local_values, on_dim):
+    latest = list(local_values.shape[1:])
+    latest[on_dim] *= local_values.shape[0]
+    return jnp.moveaxis(local_values, 0, on_dim).reshape(latest)
+
+
+def refer_flows(xx, mesh_name, k_dim):
+    full_n = lax.axis_size(mesh_name)
+    steps_seen = tuple(((u, (u + 1) % full_n) for u in range(full_n)))
+    h_now, state_next = ([], [])
+    ix = 0
+    items = tuple(((idx, hop_no) for hop_no, idx in steps_seen))
+    while ix < full_n - 1:
+        if ix % 2 == 0:
+            h_now.append(lax.ppermute(h_now[-1] if h_now else xx, mesh_name, steps_seen))
+        else:
+            reached = lax.ppermute(state_next[-1] if state_next else xx, mesh_name, items)
+            state_next.append(reached)
+        ix = ix + 1
+    z1 = jnp.stack([*h_now[::-1], xx, *state_next])
+    block_next = lax.axis_index(mesh_name)
+    known = block_next - len(h_now)
+    z1 = z1[(jnp.arange(full_n) - known) % full_n]
+    return track_packet_for(z1, k_dim)
+
+
+hold_flows = functools.partial(refer_flows, mesh_name="fsdp", k_dim=0)
 
 
 def inverse_rms(vector):
@@ -181,9 +211,7 @@
     slot_inputs = jnp.where(filled[:, None], normed_two[owner_rows // TOPK], zero_half).reshape(
         E, CAP, D
     )
-    produced, gate_pre, up_pre = expert_forward(
-        slot_inputs, lax.all_gather(expert_weights, "fsdp", axis=0, tiled=True)
-    )
+    produced, gate_pre, up_pre = expert_forward(slot_inputs, hold_flows(expert_weights))
     picked = produced.reshape(E * CAP, D)[slot_ids].reshape(tokens, TOPK, D)
     mixture = jnp.einsum("tk,tkd->td", gate_probs, picked, preferred_element_type=jnp.float32)
     layer_out = (after + residual_scale * mixture).astype(jnp.bfloat16)

time: 2160 us -> 2740 us (1.27)
  blocking collectives: 59.8 us -> 361 us
  waiting for transfers between devices: 1710 us -> 1830 us
  local copies, waits for them, and re-layouts: 90.1 us -> 209 us
  other arithmetic: 89.7 us -> 125 us
    ppermute x0 -> x7, waiting for transfers between devices: none -> 566 us  [the longest x4 535 us: refer_flows(): lax.ppermute(h_now[-1] if h_now else xx, mesh_name, steps_seen)]
    all_gather x1, waiting for transfers between devices: 416 us -> 0.01 us  [body(): lax.all_gather(expert_weights, 'fsdp', axis=0, tiled=True)]
    all_gather x1, blocking collectives: 13.5 us -> 314 us  [body(): lax.all_gather(norm1_gain, 'fsdp', axis=0, tiled=True)]
    gather x0 -> x5, local copies, waits for them, and re-layouts: none -> 76.7 us  [refer_flows(): z1 = z1[(jnp.arange(full_n) - known) % full_n]]
    unnamed x127 -> x164, local copies, waits for them, and re-layouts: 29 us -> 69.5 us
    reduce_scatter x1, waiting for transfers between devices: 0.02 us -> 34.5 us  [body(): lax.psum_scatter(grad_output_w, 'fsdp', scatter_dimension=0, tiled=True)]
    unnamed x0 -> x3, other arithmetic: none -> 32.7 us
  transfers between devices with their start and end apart: 12 -> 19, of which waited for: 7 -> 8; matrix products, arithmetic and copies ran while one was open for 9% -> 15% of each run, Pallas kernels for 0% -> 0%
where the time goes in v1:
time: 2740 us; the launch traced here: 2730 us
  waiting for transfers between devices  1830 us (67%)
  blocking collectives  361 us (13%)
  local copies, waits for them, and re-layouts  209 us (8%)
  matrix products  181 us (7%)
  other arithmetic  125 us (5%)
    reduce_scatter x1, waiting for transfers between devices, body(): lax.psum_scatter(expert_grads(slot_inputs, slot_grads, gate_pre, up_pre,...  955 us
    ppermute x4, waiting for transfers between devices, refer_flows(): lax.ppermute(h_now[-1] if h_now else xx, mesh_name, steps_seen)  535 us
    all_gather x1, blocking collectives, body(): lax.all_gather(norm1_gain, 'fsdp', axis=0, tiled=True)  314 us
    psum x1, waiting for transfers between devices, body(): lax.psum((shard_gain_one, shard_query, shard_key, shard_value, shard_outp...  258 us
    gather x5, local copies, waits for them, and re-layouts, refer_flows(): z1 = z1[(jnp.arange(full_n) - known) % full_n]  76.7 us
    unnamed x164, local copies, waits for them, and re-layouts  69.5 us
    concatenate x1, other arithmetic, expert_grads(): jnp.concatenate([jnp.einsum('ecf,ecd->efd', grad_gate, slot_inputs, prefe...  66.8 us
  transfers between devices with their start and end apart: 19, of which 8 were waited for; matrix products, arithmetic and copies ran while one was open for 15% of the time, Pallas kernels for 0%

profile of v1, /device:TPU:0, one launch (start us, length us, event | category | flops | bytes accessed | tf_op | source)
XLA Modules:
  0.0 2727.6 jit_solution(15474203655853255074)
XLA Ops:
  11.2 81.3 %collective-permute-done = bf16[2,1536,1024]{2,1,0:T(8,128)(2,1)S(1)} collective-permute-done((bf16[2,1536,1024]{2,1,0:T(8,128)(2,1)}, bf16[2,1536,1024]{2,1,0:T(8,128)(2,1)S(1)}, u32[]{:S(2)}, u32[]{:S(2)}) %collective-permute-start) | collective-permute-done | bytes 6291488 | tf_op jit(solution)/shard_map/ppermute | solution.py:36
  95.2 3.5 collective-permute-start.4
  98.8 214.6 %collective-permute-done.1 = bf16[2,1536,1024]{2,1,0:T(8,128)(2,1)} collective-permute-done((bf16[2,1536,1024]{2,1,0:T(8,128)(2,1)S(1)}, bf16[2,1536,1024]{2,1,0:T(8,128)(2,1)}, u32[]{:S(2)}, u32[]{:S(2)}) %collective-permute-start.1) | collective-permute-done | bytes 6291488 | tf_op jit(solution)/shard_map/ppermute | solution.py:36
  314.2 4.5 reduce-window.19
  319.6 8.1 scatter_custom_fusion
  327.9 3.6 collective-permute-start.5
  331.5 239.2 %collective-permute-done.2 = bf16[2,1536,1024]{2,1,0:T(8,128)(2,1)} collective-permute-done((bf16[2,1536,1024]{2,1,0:T(8,128)(2,1)}, bf16[2,1536,1024]{2,1,0:T(8,128)(2,1)}, u32[]{:S(2)}, u32[]{:S(2)}) %collective-permute-start.2) | collective-permute-done | bytes 6291488 | tf_op jit(solution)/shard_map/ppermute | solution.py:36
  571.2 314.4 %all-gather = bf16[8,1,128]{2,1,0:T(2,128)(2,1)S(1)} all-gather(bf16[1,1,128]{2,1,0:T(2,128)(2,1)S(1)} %bitcast.231), channel_id=1, replica_groups=mesh['replica'=4,'fsdp'=8] {'fsdp'}, dimensions={0}, use_global_device_ids=true | all-gather | bytes 2304 | tf_op jit(solution)/shard_map/all_gather | solution.py:129
  885.7 8.8 all-gather.1
  894.6 12.7 all_gather.30
  927.4 8.1 gather_fusion
  937.8 6.1 bitcast_dynamic-update-slice_fusion.7
  943.9 6.3 bitcast_dynamic-update-slice_fusion.6
  950.2 6.3 bitcast_dynamic-update-slice_fusion.5
  959.9 3.5 bitcast_dynamic-update-slice_fusion.3
  963.4 6.1 bitcast_dynamic-update-slice_fusion.2
  969.5 6.1 bitcast_dynamic-update-slice_fusion.1
  975.6 30.3 %collective-permute-done.6 = bf16[2,1536,1024]{2,1,0:T(8,128)(2,1)S(1)} collective-permute-done((bf16[2,1536,1024]{2,1,0:T(8,128)(2,1)}, bf16[2,1536,1024]{2,1,0:T(8,128)(2,1)S(1)}, u32[]{:S(2)}, u32[]{:S(2)}) %collective-permute-start.6) | collective-permute-done | bytes 6291488 | tf_op jit(solution)/shard_map/ppermute | solution.py:38
  1009.4 32.9 %fusion.111 = (bf16[8,2,384,1024]{3,2,1,0:T(8,128)(2,1)}, bf16[8,2,384,1024]{3,2,1,0:T(8,128)(2,1)}, bf16[8,2,384,1024]{3,2,1,0:T(8,128)(2,1)}, bf16[8,2,384,1024]{3,2,1,0:T(8,128)(2,1)}) fusion(bf16[8,2,1536,1024]{3,2,1,0:T(8,128)(2,1)} %bitcast_dynamic-update-slice_fusion), kind=kLoop, calls=%fused_computation.205 | loop fusion | bytes 100663296 | tf_op jit(solution)/shard_map/gather | solution.py:44
  1042.3 11.0 gather_fusion.7
  1053.3 10.9 gather_fusion.6
  1064.2 10.9 gather_fusion.5
  1075.1 11.0 gather_fusion.4
  1086.1 32.7 %pad_maximum_fusion.1 = bf16[8,2,1536,1024]{3,2,1,0:T(8,128)(2,1)} fusion(bf16[8,2,384,1024]{3,2,1,0:T(8,128)(2,1)} %gather_fusion.7, bf16[8,2,384,1024]{3,2,1,0:T(8,128)(2,1)} %gather_fusion.6, bf16[8,2,384,1024]{3,2,1,0:T(8,128)(2,1)} %gather_fusion.5, bf16[8,2,384,1024]{3,2,1,0:T(8,128)(2,1)} %gather_fusion.4), kind=kLoop, calls=%fused_computation.10 | loop fusion | flops 201326592 | bytes 100663296
  1118.8 11.5 fusion.10
  1130.3 13.4 multiply_convert_fusion.2
  1143.8 11.5 fusion.26
  1155.3 14.0 gather_fusion.1
  1169.3 4.6 fusion.17
  1176.8 13.8 gather_fusion.2
  1190.6 4.5 fusion.19
  1195.0 14.4 multiply_convert_fusion.1
  1209.4 12.4 fusion
  1221.8 12.1 add_convert_fusion
  1234.0 13.9 gather_fusion.3
  1247.9 5.6 convert_reduce_fusion
  1279.8 19.2 fusion.21
  1299.0 4.0 fusion.70
  1303.0 18.5 fusion.24
  1321.5 19.1 fusion.25
  1340.6 66.8 %pad_maximum_fusion = f32[16,1536,1024]{2,1,0:T(8,128)} fusion(f32[16,512,1024]{2,1,0:T(8,128)} %fusion.21, f32[16,512,1024]{2,1,0:T(8,128)} %fusion.24, f32[16,512,1024]{2,1,0:T(8,128)} %fusion.25), kind=kLoop, calls=%fused_computation.9 | loop fusion | flops 50331648 | bytes 201326592 | tf_op jit(solution)/shard_map/concatenate | solution.py:104
  1409.4 34.5 %reduce-scatter.13.cloned.1.call-done = f32[128,1024]{1,0:T(8,128)} async-done(((f32[1024,1024]{1,0:T(8,128)}), f32[128,1024]{1,0:T(8,128)}) %reduce-scatter.13.cloned.1.call-update) | async-done | bytes 524304 | tf_op jit(solution)/shard_map/reduce_scatter | solution.py:318
  1443.9 955.4 %reduce-scatter.17.cloned.1.call-done = f32[2,1536,1024]{2,1,0:T(8,128)} async-done(((f32[16,1536,1024]{2,1,0:T(8,128)}), f32[2,1536,1024]{2,1,0:T(8,128)}) %reduce-scatter.17.cloned.1.call-update) | async-done | bytes 12582928 | tf_op jit(solution)/shard_map/reduce_scatter | solution.py:237
  2407.4 13.9 all-reduce.2
  2421.5 9.2 reduce-scatter.15.cloned.1.call-done
  2430.7 11.0 all-reduce.3
  2443.0 258.2 %all-reduce.7.cloned.1.call-done = (f32[128,1024]{1,0:T(8,128)}, f32[128,512]{1,0:T(8,128)}, f32[128,512]{1,0:T(8,128)}, f32[128,1024]{1,0:T(8,128)}, f32[2,1536,1024]{2,1,0:T(8,128)}) async-done(((f32[128,1024]{1,0:T(8,128)}, f32[128,512]{1,0:T(8,128)}, f32[128,512]{1,0:T(8,128)}, f32[128,1024]{1,0:T(8,128)}, f32[2,1536,1024]{2,1,0:T(8,128)}), (f32[128,1024]{1,0:T(8,128)}, f32[128,512]{1,0:T(8,128)}, ...) | async-done | bytes 14155792 | tf_op jit(solution)/shard_map/psum | solution.py:322
  2708.3 12.1 copy.114
  (283 shorter events, 84.7 us)
Async XLA Ops:
  7.2 306.2 %copy-start.44 = (s32[256,8]{0,1:T(8,128)S(1)}, s32[256,8]{0,1:T(8,128)}, u32[]{:S(2)}) copy-start(s32[256,8]{0,1:T(8,128)} %param.14) | copy-start | bytes 24580
  7.2 306.8 %copy-start.68 = (s32[1,4]{1,0:T(1,128)S(1)}, s32[1,4]{1,0:T(1,128)}, u32[]{:S(2)}) copy-start(s32[1,4]{1,0:T(1,128)} %param.13) | copy-start | bytes 52
  7.2 564.0 %copy-start.66 = (bf16[128]{0:T(256)(128)(2,1)S(1)}, bf16[128]{0:T(256)(128)(2,1)}, u32[]{:S(2)}) copy-start(bf16[128]{0:T(256)(128)(2,1)} %param.15) | copy-start | bytes 772
  7.2 878.5 %copy-start.67 = (bf16[128]{0:T(256)(128)(2,1)S(1)}, bf16[128]{0:T(256)(128)(2,1)}, u32[]{:S(2)}) copy-start(bf16[128]{0:T(256)(128)(2,1)} %param.20) | copy-start | bytes 772
  7.2 887.3 %copy-start.65 = (bf16[128,16]{0,1:T(8,128)(2,1)S(1)}, bf16[128,16]{0,1:T(8,128)(2,1)}, u32[]{:S(2)}) copy-start(bf16[128,16]{0,1:T(8,128)(2,1)} %param.21) | copy-start | bytes 12292
  7.2 901.4 %copy-start.4 = (bf16[256,1024]{1,0:T(8,128)(2,1)S(1)}, bf16[256,1024]{1,0:T(8,128)(2,1)}, u32[]{:S(2)}) copy-start(bf16[256,1024]{1,0:T(8,128)(2,1)} %param.12) | copy-start | bytes 1572868
  7.2 905.0 %all-gather.8.cloned.1.call-start = ((), (), s32[]{:S(2)}) async-start(), calls=%async_computation.6 | async-start | bytes 1179648 | tf_op jit(solution)/shard_map/all_gather | solution.py:132
  8.0 906.1 %all-gather.10.cloned.1.call-start = ((), (), s32[]{:S(2)}) async-start(), calls=%async_computation.7 | async-start | bytes 1179648 | tf_op jit(solution)/shard_map/all_gather | solution.py:131
  8.7 907.5 %all-gather.12.cloned.1.call-start = ((), (), s32[]{:S(2)}) async-start(), calls=%async_computation.8 | async-start | bytes 2359296 | tf_op jit(solution)/shard_map/all_gather | solution.py:130
  9.5 900.7 %copy-start.16 = (bf16[256,1024]{1,0:T(8,128)(2,1)S(1)}, bf16[256,1024]{1,0:T(8,128)(2,1)}, u32[]{:S(2)}) copy-start(bf16[256,1024]{1,0:T(8,128)(2,1)} %param.23) | copy-start | bytes 1572868
  9.5 914.2 %all-gather.14.cloned.1.call-start = ((), (), s32[]{:S(2)}) async-start(), calls=%async_computation.9 | async-start | bytes 2359296 | tf_op jit(solution)/shard_map/all_gather | solution.py:133
  10.0 1185.0 %all-gather.16.cloned.1.call-start = ((), (), s32[]{:S(2)}) async-start(), calls=%async_computation.10 | async-start | bytes 56623104 | tf_op jit(solution)/shard_map/all_gather | solution.py:235
  10.6 1398.7 %reduce-scatter.9.cloned.1.call-start = ((), (), s32[]{:S(2)}) async-start(), calls=%async_computation.12 | async-start | bytes 2359296 | tf_op jit(solution)/shard_map/reduce_scatter | solution.py:316
  10.7 81.8 %collective-permute-start = (bf16[2,1536,1024]{2,1,0:T(8,128)(2,1)}, bf16[2,1536,1024]{2,1,0:T(8,128)(2,1)S(1)}, u32[]{:S(2)}, u32[]{:S(2)}) collective-permute-start(bf16[2,1536,1024]{2,1,0:T(8,128)(2,1)} %param.22), channel_id=1, source_target_pairs={{0,1},{1,2},{2,3},{3,4},{4,5},{5,6},{6,7},{7,0},{8,9},{9,10},{10,1... | collective-permute-start | bytes 18874376 | tf_op jit(solution)/shard_map/ppermute | solution.py:36
  95.2 218.2 %collective-permute-start.1 = (bf16[2,1536,1024]{2,1,0:T(8,128)(2,1)S(1)}, bf16[2,1536,1024]{2,1,0:T(8,128)(2,1)}, u32[]{:S(2)}, u32[]{:S(2)}) collective-permute-start(bf16[2,1536,1024]{2,1,0:T(8,128)(2,1)S(1)} %collective-permute-done), channel_id=1, source_target_pairs={{0,1},{1,2},{2,3},{3,4},{4,5},{5,6},{6,7},{7,0},{8,9},{9,10},{10,1... | collective-permute-start | bytes 18874376 | tf_op jit(solution)/shard_map/ppermute | solution.py:36
  95.2 232.6 %collective-permute-start.4 = (bf16[2,1536,1024]{2,1,0:T(8,128)(2,1)}, bf16[2,1536,1024]{2,1,0:T(8,128)(2,1)}, u32[]{:S(2)}, u32[]{:S(2)}) collective-permute-start(bf16[2,1536,1024]{2,1,0:T(8,128)(2,1)} %param.22), channel_id=1, source_target_pairs={{1,0},{2,1},{3,2},{4,3},{5,4},{6,5},{7,6},{0,7},{9,8},{10,9},{11,1... | collective-permute-start | bytes 18874376 | tf_op jit(solution)/shard_map/ppermute | solution.py:38
  313.4 257.3 %collective-permute-start.2 = (bf16[2,1536,1024]{2,1,0:T(8,128)(2,1)}, bf16[2,1536,1024]{2,1,0:T(8,128)(2,1)}, u32[]{:S(2)}, u32[]{:S(2)}) collective-permute-start(bf16[2,1536,1024]{2,1,0:T(8,128)(2,1)} %collective-permute-done.1), channel_id=1, source_target_pairs={{0,1},{1,2},{2,3},{3,4},{4,5},{5,6},{6,7},{7,0},{8,9},{9,10},{10,1... | collective-permute-start | bytes 18874376 | tf_op jit(solution)/shard_map/ppermute | solution.py:36
  327.9 608.6 %collective-permute-start.5 = (bf16[2,1536,1024]{2,1,0:T(8,128)(2,1)}, bf16[2,1536,1024]{2,1,0:T(8,128)(2,1)}, u32[]{:S(2)}, u32[]{:S(2)}) collective-permute-start(bf16[2,1536,1024]{2,1,0:T(8,128)(2,1)} %collective-permute-done.4), channel_id=1, source_target_pairs={{1,0},{2,1},{3,2},{4,3},{5,4},{6,5},{7,6},{0,7},{9,8},{10,9},{11,1... | collective-permute-start | bytes 18874376 | tf_op jit(solution)/shard_map/ppermute | solution.py:38
  570.7 367.1 %collective-permute-start.3 = (bf16[2,1536,1024]{2,1,0:T(8,128)(2,1)}, bf16[2,1536,1024]{2,1,0:T(8,128)(2,1)}, u32[]{:S(2)}, u32[]{:S(2)}) collective-permute-start(bf16[2,1536,1024]{2,1,0:T(8,128)(2,1)} %collective-permute-done.2), channel_id=1, source_target_pairs={{0,1},{1,2},{2,3},{3,4},{4,5},{5,6},{6,7},{7,0},{8,9},{9,10},{10,1... | collective-permute-start | bytes 18874376 | tf_op jit(solution)/shard_map/ppermute | solution.py:36
  885.7 30.5 %copy-start.41 = (f32[8,1,128]{2,1,0:T(1,128)}, f32[8,1,128]{2,1,0:T(1,128)S(1)}, u32[]{:S(2)}) copy-start(f32[8,1,128]{2,1,0:T(1,128)S(1)} %convert_element_type.151) | copy-start | bytes 12292
  894.5 32.4 %copy-start.51 = (f32[8,1,128]{2,1,0:T(1,128)}, f32[8,1,128]{2,1,0:T(1,128)S(1)}, u32[]{:S(2)}) copy-start(f32[8,1,128]{2,1,0:T(1,128)S(1)} %convert_element_type.152) | copy-start | bytes 12292
  907.3 28.2 %copy-start.37 = (bf16[1024,16]{0,1:T(8,128)(2,1)}, bf16[1024,16]{0,1:T(8,128)(2,1)S(1)}, u32[]{:S(2)}) copy-start(bf16[1024,16]{0,1:T(8,128)(2,1)S(1)} %all_gather.30) | copy-start | bytes 98308
  908.7 10.3 copy-start.33
  914.1 7.3 copy-start.32
  923.6 11.9 copy-start.30
  926.9 8.6 copy-start.58
  927.4 8.1 copy-start
  935.8 8.1 copy-start.46
  935.9 8.0 copy-start.60
  936.4 69.5 %collective-permute-start.6 = (bf16[2,1536,1024]{2,1,0:T(8,128)(2,1)}, bf16[2,1536,1024]{2,1,0:T(8,128)(2,1)S(1)}, u32[]{:S(2)}, u32[]{:S(2)}) collective-permute-start(bf16[2,1536,1024]{2,1,0:T(8,128)(2,1)} %collective-permute-done.5), channel_id=1, source_target_pairs={{1,0},{2,1},{3,2},{4,3},{5,4},{6,5},{7,6},{0,7},{9,8},{10,9},{11,1... | collective-permute-start | bytes 18874376 | tf_op jit(solution)/shard_map/ppermute | solution.py:38
  943.9 12.6 slice-start.2
  950.2 9.7 slice-start
  1143.8 11.5 copy-start.14
  1143.8 11.5 copy-start.50
  1155.3 14.0 copy-start.36
  1176.7 13.8 copy-start.45
  1190.5 63.0 %copy-start.48 = (bf16[256,16]{0,1:T(8,128)(2,1)}, bf16[256,16]{0,1:T(8,128)(2,1)S(1)}, u32[]{:S(2)}) copy-start(bf16[256,16]{0,1:T(8,128)(2,1)S(1)} %select_reduce_fusion) | copy-start | bytes 24580
  1209.4 12.4 copy-start.7
  1247.9 6.9 copy-start.17
  1267.6 141.7 %reduce-scatter.11.cloned.1.call-start = ((), (), s32[]{:S(2)}) async-start(), calls=%async_computation.13 | async-start | bytes 2359296 | tf_op jit(solution)/shard_map/reduce_scatter | solution.py:317
  1273.3 136.1 %reduce-scatter.7.cloned.1.call-start = ((), (), s32[]{:S(2)}) async-start(), calls=%async_computation.11 | async-start | bytes 4718592 | tf_op jit(solution)/shard_map/reduce_scatter | solution.py:315
  1279.5 19.5 copy-start.31
  1279.5 164.4 %reduce-scatter.13.cloned.1.call-start = ((), (), s32[]{:S(2)}) async-start(), calls=%async_computation.14 | async-start | bytes 4718592 | tf_op jit(solution)/shard_map/reduce_scatter | solution.py:318
  1302.9 1096.4 %reduce-scatter.17.cloned.1.call-start = ((), (), s32[]{:S(2)}) async-start(), calls=%async_computation.16 | async-start | bytes 113246208 | tf_op jit(solution)/shard_map/reduce_scatter | solution.py:237
  1407.4 1023.2 %reduce-scatter.15.cloned.1.call-start = ((), (), s32[]{:S(2)}) async-start(), calls=%async_computation.15 | async-start | bytes 73728 | tf_op jit(solution)/shard_map/reduce_scatter | solution.py:320
  1409.3 1291.9 %all-reduce.7.cloned.1.call-start = ((), (), s32[]{:S(2)}) async-start(), calls=%async_computation.17 | async-start | bytes 28311552 | tf_op jit(solution)/shard_map/psum | solution.py:322
  2401.2 40.5 %copy-start.10 = (f32[256,1024]{1,0:T(8,128)S(1)}, f32[256,1024]{1,0:T(8,128)}, u32[]{:S(2)}) copy-start(f32[256,1024]{1,0:T(8,128)} %copy-done.9) | copy-start | bytes 3145732
  2401.2 40.5 %copy-start.62 = (f32[256]{0:T(256)S(1)}, f32[256]{0:T(256)}, u32[]{:S(2)}) copy-start(f32[256]{0:T(256)} %get-tuple-element.50) | copy-start | bytes 3076
  (45 other events, 154.5 us)
Sparse Core Ops, SparseCore 0:
  9.7 84.3 all-gather.7
  95.7 26.3 all-gather.9
  123.7 42.9 all-gather.11
  168.1 45.5 all-gather.13
  215.2 671.0 all-gather.15
  1267.8 37.0 reduce-scatter.8
  1307.1 34.5 reduce-scatter.10
  1344.6 48.7 reduce-scatter.6
  1395.7 48.1 reduce-scatter.12
  1446.1 953.1 reduce-scatter.16
  2402.2 28.3 reduce-scatter.14
  2434.9 266.2 all-reduce.6
